TPU v7x, 32 devices: a whole 2x2x4 slice. The times are simulated.
32 devices in a mesh: gx: 2 (over x), yz: 16 (over z, y, core).
Axes of the slice: x: 2, y: 2, z: 4, core: 2. Of those that a mesh axis runs over, the one named last changes fastest.
Arguments:
- tensor: float32 [4, 512, 32, 32], P(None, 'gx', 'yz'), may hold values from -40 to 40
- start_basis: float32 [96, 512], replicated, may hold values from -6 to 6
Outputs:
- core_tensor: float32 [32, 32, 384], P(('gx', 'yz'))
- factor: float32 [96, 512], replicated
All inputs are finite; a program needn't handle non-finite values.
Results may differ from a plain program's by a relative error of at most 0.00012.
Values sent between devices are 32-bit elements; how exact they have to be, the bound alone decides.
A program may use at most 64 MiB of HBM per device.

v0:
```python
import functools

import jax
import jax.numpy as jnp
from jax import lax
from jax.experimental import pallas as pl
from jax.experimental.pallas import tpu as pltpu
from jax.sharding import PartitionSpec as P

HIGHEST = lax.Precision.HIGHEST
LANES = 128
SUBLANES = 8


def mm(a, b):
    return lax.dot_general(
        a, b, (((1,), (0,)), ((), ())), precision=HIGHEST, preferred_element_type=jnp.float32
    )


def mm_nt(a, b):
    return lax.dot_general(
        a, b, (((1,), (1,)), ((), ())), precision=HIGHEST, preferred_element_type=jnp.float32
    )


def inverse_cholesky(gram, panel=SUBLANES):
    rank = gram.shape[0]
    wide = -(-rank // LANES) * LANES
    row_id = lax.broadcasted_iota(jnp.int32, (rank, wide), 0)
    lane_id = lax.broadcasted_iota(jnp.int32, (rank, wide), 1)
    left = jnp.concatenate([gram, jnp.zeros((rank, wide - rank), jnp.float32)], axis=1) if wide > rank else gram
    right = jnp.where(row_id == lane_id, 1.0, 0.0).astype(jnp.float32)
    done_right, done_pivots = [], []
    for base in range(0, rank, SUBLANES):
        rows = rank - base
        local_row = lax.broadcasted_iota(jnp.int32, (rows, wide), 0)
        pivots = jnp.zeros((SUBLANES, wide), jnp.float32)
        for first in range(0, SUBLANES, panel):
            spread = [
                jnp.broadcast_to(left[:, base + step : base + step + 1], (rows, wide))
                for step in range(first, first + panel)
            ]
            for step in range(first, first + panel):
                column = spread[step - first]
                pivot = column[step : step + 1]
                pivots = jnp.where(local_row[:SUBLANES] == step, jnp.broadcast_to(pivot, (SUBLANES, wide)), pivots)
                factor = jnp.where(local_row > step, column * (1.0 / pivot), 0.0)
                for other in range(step + 1, first + panel):
                    spread[other - first] = spread[other - first] - factor * spread[other - first][step : step + 1]
                left = left - factor * left[step : step + 1]
                right = right - factor * right[step : step + 1]
        done_right.append(right[:SUBLANES] / jnp.sqrt(pivots))
        left, right = left[SUBLANES:], right[SUBLANES:]
    return jnp.concatenate(done_right, axis=0)[:, :rank]


def kernel(
    shape,
    x_ref,
    start_ref,
    core_ref,
    factor_ref,
    xg,
    stage,
    sums,
    pairs,
    parts,
    core_out,
    core_in,
    x_send,
    x_recv,
    send_sem,
    recv_sem,
):
    n_gx, n_yz, cell_count, rows = shape
    n = n_gx * n_yz
    my_x, my_yz = lax.axis_index("gx"), lax.axis_index("yz")
    me = my_x * n_yz + my_yz
    species, _, cells_z, width = x_ref.shape
    lines = xg.shape[2]
    rank, total = start_ref.shape
    per_column = rank // rows
    order = range(n - 1, 0, -1)
    odds = range(n - 1, 0, -2)
    direct = [*range(n - 2, 0, -2), 1]
    flips = [1 - 2 * lax.rem(lax.div(me, 1 << bit), 2) for bit in range(n.bit_length() - 1)]

    def place(flat):
        return {"gx": lax.div(flat, n_yz), "yz": lax.rem(flat, n_yz)}

    def partner(k):
        return me + sum((1 << bit) * flip for bit, flip in enumerate(flips) if k >> bit & 1)

    barrier = pltpu.get_barrier_semaphore()

    for k in order:
        pl.semaphore_signal(barrier, inc=1, device_id=place(partner(k)), device_id_type=pl.DeviceIdType.MESH)

    xg[my_x] = x_ref[:, pl.ds(my_x * lines, lines)]
    pl.semaphore_wait(barrier, n - 1)

    def x_copy(k):
        peer = lax.rem(my_x + k, n_gx)
        return pltpu.make_async_remote_copy(
            src_ref=x_ref.at[:, pl.ds(peer * lines, lines)],
            dst_ref=xg.at[my_x],
            send_sem=x_send.at[k - 1],
            recv_sem=x_recv.at[k - 1],
            device_id={"gx": peer, "yz": my_yz},
            device_id_type=pl.DeviceIdType.MESH,
        )

    for k in range(1, n_gx):
        x_copy(k).start()
    for k in range(1, n_gx):
        x_copy(k).wait()

    def held(part):
        return xg[part].reshape(species * lines * cells_z, width)

    def image_of(basis):
        projected = None
        for part in range(n_gx):
            term = mm_nt(basis[:, part * width : (part + 1) * width], held(part))
            projected = term if projected is None else projected + term
        projected = projected * (1.0 / cell_count)
        return jnp.concatenate([mm(projected, held(part)) for part in range(n_gx)], axis=1)

    def scatter_copy(turn, k):
        odd = k % 2
        return pltpu.make_async_remote_copy(
            src_ref=stage.at[turn, partner(k)],
            dst_ref=pairs.at[turn, k // 2] if odd else parts.at[turn, k // 2 - 1],
            send_sem=send_sem.at[2 * turn, k - 1],
            recv_sem=recv_sem.at[2 * turn, k - 1],
            device_id=place(partner(1) if odd else partner(k)),
            device_id_type=pl.DeviceIdType.MESH,
        )

    def gather_copy(turn, k):
        return pltpu.make_async_remote_copy(
            src_ref=sums.at[turn, me],
            dst_ref=sums.at[turn, me],
            send_sem=send_sem.at[2 * turn + 1, k - 1],
            recv_sem=recv_sem.at[2 * turn + 1, k - 1],
            device_id=place(partner(k)),
            device_id_type=pl.DeviceIdType.MESH,
        )

    def relay_copy(turn, k):
        source = partner(k)
        return pltpu.make_async_remote_copy(
            src_ref=sums.at[turn, source],
            dst_ref=sums.at[turn, source],
            send_sem=send_sem.at[2 * turn + 1, k],
            recv_sem=recv_sem.at[2 * turn + 1, k],
            device_id=place(partner(1)),
            device_id_type=pl.DeviceIdType.MESH,
        )

    def gather_arrival(turn, k):
        source = partner(k)
        return pltpu.make_async_remote_copy(
            src_ref=sums.at[turn, me],
            dst_ref=sums.at[turn, source],
            send_sem=send_sem.at[2 * turn + 1, k - 1],
            recv_sem=recv_sem.at[2 * turn + 1, k - 1],
            device_id=place(partner(k)),
            device_id_type=pl.DeviceIdType.MESH,
        )

    def start_scatter(turn, image):
        for owner in range(n):
            column, block = owner // per_column, owner % per_column
            stage[turn, owner] = image[block * rows : (block + 1) * rows, column * LANES : (column + 1) * LANES]
        for k in odds:
            scatter_copy(turn, k).start()
        for k in odds:
            scatter_copy(turn, k).wait_recv()
            stage[turn, partner(k - 1)] = stage[turn, partner(k - 1)] + pairs[turn, k // 2]
            if k > 1:
                scatter_copy(turn, k - 1).start()

    def start_gather(turn):
        for k in odds[:-1]:
            scatter_copy(turn, k - 1).wait_recv()
        terms = [stage[turn, me]] + [parts[turn, k] for k in range(n // 2 - 1)]
        while len(terms) > 1:
            terms = [a + b for a, b in zip(terms[::2], terms[1::2])] + ([terms[-1]] if len(terms) % 2 else [])
        sums[turn, me] = terms[0]
        for k in direct:
            gather_copy(turn, k).start()
        for k in order:
            scatter_copy(turn, k).wait_send()

    def gathered(turn):
        for k in direct:
            gather_arrival(turn, k).wait_recv()
            if k > 1:
                relay_copy(turn, k).start()
        for k in direct:
            if k > 1:
                relay_copy(turn, k).wait_recv()
        blocks = [sums[turn, owner] for owner in range(n)]
        columns = [jnp.concatenate(blocks[at : at + per_column], axis=0) for at in range(0, n, per_column)]
        return jnp.concatenate(columns, axis=1)

    start_scatter(0, image_of(start_ref[...]))
    start_gather(0)
    image = gathered(0)
    start_scatter(1, image_of(image))
    start_gather(1)
    inverse = inverse_cholesky(mm_nt(image, image))
    image = mm(inverse, gathered(1))
    basis = mm(inverse_cholesky(mm_nt(image, image)), image)
    factor_ref[...] = basis

    truncated = None
    for part in range(n_gx):
        term = mm_nt(held(part), basis[:, part * width : (part + 1) * width])
        truncated = term if truncated is None else truncated + term
    share = cells_z // n
    for s in range(species):
        for line in range(lines):
            at = (s * lines + line) * cells_z
            core_out[:, line, s * rank : (s + 1) * rank] = truncated[at : at + cells_z]

    mine = my_yz * n_gx + my_x

    def core_copy(k):
        peer = partner(k)
        return pltpu.make_async_remote_copy(
            src_ref=core_out.at[pl.ds(peer * share, share)],
            dst_ref=core_in.at[mine],
            send_sem=send_sem.at[4, k - 1],
            recv_sem=recv_sem.at[4, k - 1],
            device_id=place(peer),
            device_id_type=pl.DeviceIdType.MESH,
        )

    def core_arrival(k):
        source = partner(k)
        place_of = lax.rem(source, n_yz) * n_gx + lax.div(source, n_yz)
        return pltpu.make_async_remote_copy(
            src_ref=core_out.at[pl.ds(partner(k) * share, share)],
            dst_ref=core_in.at[place_of],
            send_sem=send_sem.at[4, k - 1],
            recv_sem=recv_sem.at[4, k - 1],
            device_id=place(partner(k)),
            device_id_type=pl.DeviceIdType.MESH,
        )

    for k in order:
        core_copy(k).start()

    core_in[mine] = core_out[pl.ds(me * share, share)]

    for k in order:
        for turn in range(2):
            if k in direct:
                gather_copy(turn, k).wait_send()
            else:
                relay_copy(turn, k - 1).wait_send()
        core_arrival(k).wait()

    core_ref[...] = core_in[...]


def kernel_program(tensor, start_basis, n_gx, n_yz, rows):
    n = n_gx * n_yz
    species, width, lines_held, cells_z = tensor.shape
    rank, total = start_basis.shape
    lines = lines_held // n_gx
    cell_count = species * lines_held * n_yz * cells_z
    share = cells_z // n
    out = species * rank
    core, factor = pl.pallas_call(
        functools.partial(kernel, (n_gx, n_yz, cell_count, rows)),
        out_shape=(
            pltpu.VMEM((n, share, lines, out), jnp.float32),
            pltpu.VMEM((rank, total), jnp.float32),
        ),
        in_specs=[pl.BlockSpec(memory_space=pltpu.VMEM)] * 2,
        out_specs=(pl.BlockSpec(memory_space=pltpu.VMEM),) * 2,
        scratch_shapes=[
            pltpu.VMEM((n_gx, species, lines, cells_z, width), jnp.float32),
            pltpu.VMEM((2, n, rows, LANES), jnp.float32),
            pltpu.VMEM((2, n, rows, LANES), jnp.float32),
            pltpu.VMEM((2, n // 2, rows, LANES), jnp.float32),
            pltpu.VMEM((2, n // 2 - 1, rows, LANES), jnp.float32),
            pltpu.VMEM((cells_z, lines, out), jnp.float32),
            pltpu.VMEM((n, share, lines, out), jnp.float32),
            pltpu.SemaphoreType.DMA((n_gx - 1,)),
            pltpu.SemaphoreType.DMA((n_gx - 1,)),
            pltpu.SemaphoreType.DMA((5, n - 1)),
            pltpu.SemaphoreType.DMA((5, n - 1)),
        ],
        compiler_params=pltpu.CompilerParams(collective_id=0, has_side_effects=True),
    )(tensor.transpose(0, 2, 3, 1), start_basis)
    core = core.transpose(1, 0, 2, 3).reshape(share, n * lines, out)
    return core, factor


def orthonormal(image_rows):
    small_gram = jnp.dot(image_rows, image_rows.T, precision=HIGHEST)
    lower_factor = jnp.linalg.cholesky(small_gram)
    return lax.linalg.triangular_solve(lower_factor, image_rows, left_side=True, lower=True)


def collective_program(tensor, start_basis):
    regrouped = lax.all_to_all(tensor, "gx", split_axis=2, concat_axis=1, tiled=True)
    species, _, lines, cells_z = regrouped.shape
    cell_count = species * lines * lax.axis_size("gx") * lax.axis_size("yz") * cells_z
    gram_matrix = lax.dot_general(
        regrouped, regrouped, (((0, 2, 3), (0, 2, 3)), ((), ())), precision=HIGHEST
    )
    gram_matrix = lax.psum(gram_matrix, ("gx", "yz")) / cell_count
    basis = start_basis
    for _ in range(2):
        basis = orthonormal(jnp.dot(basis, gram_matrix, precision=HIGHEST))
    core_local = jnp.einsum("kx,sxyz->zysk", basis, regrouped, precision=HIGHEST)
    core_local = core_local.reshape(cells_z, lines, species * basis.shape[0])
    core_tensor = lax.all_to_all(
        lax.all_to_all(core_local, "gx", split_axis=0, concat_axis=1, tiled=True),
        "yz",
        split_axis=0,
        concat_axis=1,
        tiled=True,
    )
    return core_tensor, basis


def solution(mesh):
    n_gx, n_yz = mesh.shape["gx"], mesh.shape["yz"]
    n = n_gx * n_yz

    def local(tensor, start_basis):
        rank, total = start_basis.shape
        rows, left_over = divmod(rank * (total // LANES), n)
        whole_rows = left_over == 0 and total % LANES == 0 and n & (n - 1) == 0
        whole_rows = whole_rows and rank % max(rows, 1) == 0 and rank % SUBLANES == 0
        if whole_rows and tensor.shape[1] % LANES == 0:
            return kernel_program(tensor, start_basis, n_gx, n_yz, rows)
        return collective_program(tensor, start_basis)

    return jax.shard_map(
        local,
        mesh=mesh,
        in_specs=(P(None, "gx", "yz", None), P()),
        out_specs=(P(("gx", "yz"), None, None), P()),
        check_vma=False,
    )
```

profile of v0, /device:TPU:0, one launch (start us, length us, event | category | flops | bytes accessed | tf_op | source)
XLA Modules:
  0.0 48.5 jit_solution(3703095252934936199)
XLA Ops:
  0.6 46.6 %shard_map.41 = (f32[32,1,1,384]{3,2,1,0:T(1,128)S(1)}, f32[96,512]{1,0:T(8,128)S(1)}) custom-call(f32[4,2,32,256]{3,2,1,0:T(8,128)} %bitcast.3, f32[96,512]{1,0:T(8,128)} %start_ref.1), custom_call_target="tpu_custom_call" | custom-call | tf_op jit(solution)/shard_map/pallas_call | solution.py:278
  47.2 0.6 %copy.4 = f32[1,32,384]{2,1,0:T(8,128)} copy(f32[1,32,384]{2,0,1:T(1,128)S(1)} %bitcast.2) | data formatting | bytes 98304
  47.9 0.7 %copy.6 = f32[96,512]{1,0:T(8,128)} copy(f32[96,512]{1,0:T(8,128)S(1)} %get-tuple-element.9) | data formatting | bytes 393216
where the time goes:
time: 48.7 us; the launch traced here: 48.5 us
  Pallas kernels  46.6 us (96%)
  local copies, waits for them, and re-layouts  1.3 us (3%)
  between operations  0.64 us (1%)
    pallas_call x1, Pallas kernels, kernel_program(): pl.pallas_call(functools.partial(kernel, (n_gx, n_yz, cell_count, rows)),...  46.6 us
    unnamed x2, local copies, waits for them, and re-layouts  1.3 us

commit v1 on v0

v1 whole, which is shorter than its diff:
```python
import functools

import jax
import jax.numpy as jnp
from jax import lax
from jax.experimental import pallas as pl
from jax.experimental.pallas import tpu as pltpu
from jax.sharding import PartitionSpec as P

HIGHEST = lax.Precision.HIGHEST
MESH = pl.DeviceIdType.MESH
LANES = 128
SUBLANES = 8


def mm(a, b):
    return lax.dot_general(
        a, b, (((1,), (0,)), ((), ())), precision=HIGHEST, preferred_element_type=jnp.float32
    )


def mm_nt(a, b):
    return lax.dot_general(
        a, b, (((1,), (1,)), ((), ())), precision=HIGHEST, preferred_element_type=jnp.float32
    )


def inverse_cholesky(gram, panel=SUBLANES):
    rank = gram.shape[0]
    wide = -(-rank // LANES) * LANES
    row_id = lax.broadcasted_iota(jnp.int32, (rank, wide), 0)
    lane_id = lax.broadcasted_iota(jnp.int32, (rank, wide), 1)
    left = jnp.concatenate([gram, jnp.zeros((rank, wide - rank), jnp.float32)], axis=1) if wide > rank else gram
    right = jnp.where(row_id == lane_id, 1.0, 0.0).astype(jnp.float32)
    done_right = []
    for base in range(0, rank, SUBLANES):
        rows = rank - base
        local_row = lax.broadcasted_iota(jnp.int32, (rows, wide), 0)
        pivots = jnp.zeros((SUBLANES, wide), jnp.float32)
        for first in range(0, SUBLANES, panel):
            spread = [
                jnp.broadcast_to(left[:, base + step : base + step + 1], (rows, wide))
                for step in range(first, first + panel)
            ]
            for step in range(first, first + panel):
                column = spread[step - first]
                pivot = column[step : step + 1]
                pivots = jnp.where(local_row[:SUBLANES] == step, jnp.broadcast_to(pivot, (SUBLANES, wide)), pivots)
                factor = jnp.where(local_row > step, column * (1.0 / pivot), 0.0)
                for other in range(step + 1, first + panel):
                    spread[other - first] = spread[other - first] - factor * spread[other - first][step : step + 1]
                left = left - factor * left[step : step + 1]
                right = right - factor * right[step : step + 1]
        done_right.append(right[:SUBLANES] / jnp.sqrt(pivots))
        left, right = left[SUBLANES:], right[SUBLANES:]
    return jnp.concatenate(done_right, axis=0)[:, :rank]


def kernel(
    shape,
    x_hbm,
    start_hbm,
    core_ref,
    factor_ref,
    xf,
    start,
    stage,
    parts,
    sums,
    core_out,
    local_sem,
    x_send,
    x_recv,
    relay_send,
    relay_recv,
    sum_send,
    sum_recv,
    all_send,
    all_recv,
    pair_send,
    pair_recv,
    core_send,
    core_recv,
):
    n_gx, n_yz, cell_count = shape
    n = n_gx * n_yz
    my_x, my_yz = lax.axis_index("gx"), lax.axis_index("yz")
    me = my_x * n_yz + my_yz
    core = lax.rem(my_yz, 2)
    mine = lax.div(me, 2)
    other_x = 1 - my_x
    _, _, species, lines, cells_z, width = xf.shape
    half = start.shape[1]
    rank = 2 * half
    owners, rows = stage.shape[1:3]
    per_column = half // rows
    held_cells = species * lines * cells_z
    flips = [1 - 2 * lax.rem(lax.div(me, 1 << bit), 2) for bit in range(n.bit_length() - 1)]
    peers = range(n - 2, 0, -2)

    def place(flat):
        return {"gx": lax.div(flat, n_yz), "yz": lax.rem(flat, n_yz)}

    def partner(k):
        return me + sum((1 << bit) * flip for bit, flip in enumerate(flips) if k >> bit & 1)

    def remote(src, dst, send, recv, k):
        return pltpu.make_async_remote_copy(
            src_ref=src, dst_ref=dst, send_sem=send, recv_sem=recv, device_id=place(partner(k)), device_id_type=MESH
        )

    barrier = pltpu.get_barrier_semaphore()
    across = n_yz
    for k in [across, 1, *(k for k in range(n - 1, 0, -1) if k not in (across, 1))]:
        pl.semaphore_signal(barrier, inc=1, device_id=place(partner(k)), device_id_type=MESH)

    kept = pl.ds(my_x * lines, lines)
    given = pl.ds(other_x * lines, lines)
    own_copy = pltpu.make_async_copy(x_hbm.at[:, kept], xf.at[my_x, 0], local_sem.at[0])
    own_copy.start()
    mine_rows = pl.ds(pl.multiple_of(core * half, SUBLANES), half)
    start_copies = [
        pltpu.make_async_copy(
            start_hbm.at[mine_rows, part * width : (part + 1) * width], start.at[part], local_sem.at[1 + part]
        )
        for part in range(n_gx)
    ]
    for copy in start_copies:
        copy.start()

    with jax.named_scope("s_barrier"):
        pl.semaphore_wait(barrier, n - 1)

    x_copies = [
        remote(x_hbm.at[s, given], xf.at[my_x, 0, s], x_send.at[s], x_recv.at[s], across) for s in range(species)
    ]
    x_arrivals = [
        remote(x_hbm.at[s, given], xf.at[other_x, 0, s], x_send.at[s], x_recv.at[s], across) for s in range(species)
    ]
    kept_copy = remote(x_hbm.at[:, kept], xf.at[my_x, 1], relay_send.at[species], relay_recv.at[species], 1)
    relays = [
        remote(xf.at[other_x, 0, s], xf.at[other_x, 1, s], relay_send.at[s], relay_recv.at[s], 1)
        for s in range(species)
    ]

    def cells(part, side):
        return xf[part, side].reshape(held_cells, width)

    with jax.named_scope("s_xex"):
        for copy in x_copies:
            copy.start()
        kept_copy.start()
        own_copy.wait()
        for copy in start_copies:
            copy.wait()
        kept_copy.wait_recv()
        projected = [mm_nt(start[my_x], cells(my_x, side)) for side in range(2)]
        for arrival, relay in zip(x_arrivals, relays):
            arrival.wait_recv()
            relay.start()
        projected[0] = projected[0] + mm_nt(start[other_x], cells(other_x, 0))
        for relay in relays:
            relay.wait_recv()
        projected[1] = projected[1] + mm_nt(start[other_x], cells(other_x, 1))

    def image_of(projected):
        projected = [term * (1.0 / cell_count) for term in projected]
        columns = [sum(mm(projected[side], cells(part, side)) for side in range(2)) for part in range(n_gx)]
        return jnp.concatenate(columns, axis=1)

    def sum_copy(turn, k):
        return remote(
            stage.at[turn, lax.div(partner(k), 2)],
            parts.at[turn, k // 2 - 1],
            sum_send.at[turn, k // 2 - 1],
            sum_recv.at[turn, k // 2 - 1],
            k,
        )

    def all_copy(turn, k):
        return remote(
            sums.at[turn, core, mine],
            sums.at[turn, core, mine],
            all_send.at[turn, k // 2 - 1],
            all_recv.at[turn, k // 2 - 1],
            k,
        )

    def all_arrival(turn, k):
        return remote(
            sums.at[turn, core, mine],
            sums.at[turn, core, lax.div(partner(k), 2)],
            all_send.at[turn, k // 2 - 1],
            all_recv.at[turn, k // 2 - 1],
            k,
        )

    def pair_copy(turn, k):
        block = lax.div(partner(k), 2)
        return remote(
            sums.at[turn, core, block],
            sums.at[turn, core, block],
            pair_send.at[turn, k // 2],
            pair_recv.at[turn, k // 2],
            1,
        )

    def pair_arrival(turn, k):
        block = lax.div(partner(k), 2)
        return remote(
            sums.at[turn, core, block],
            sums.at[turn, 1 - core, block],
            pair_send.at[turn, k // 2],
            pair_recv.at[turn, k // 2],
            1,
        )

    def spread(turn, image):
        for owner in range(owners):
            column, block = owner // per_column, owner % per_column
            stage[turn, owner] = image[block * rows : (block + 1) * rows, column * LANES : (column + 1) * LANES]
        for k in peers:
            sum_copy(turn, k).start()

    def total(turn):
        terms = [stage[turn, mine]]
        for k in reversed(peers):
            sum_copy(turn, k).wait_recv()
            terms.append(parts[turn, k // 2 - 1])
        while len(terms) > 1:
            terms = [a + b for a, b in zip(terms[::2], terms[1::2])] + ([terms[-1]] if len(terms) % 2 else [])
        sums[turn, core, mine] = terms[0]
        for k in peers:
            all_copy(turn, k).start()
        pair_copy(turn, 0).start()

    def gathered(turn, side):
        blocks = [sums[turn, side, owner] for owner in range(owners)]
        columns = [jnp.concatenate(blocks[at : at + per_column], axis=0) for at in range(0, owners, per_column)]
        return jnp.concatenate(columns, axis=1)

    def collect(turn):
        for k in reversed(peers):
            all_arrival(turn, k).wait_recv()
            pair_copy(turn, k).start()

    def whole(turn):
        for k in [0, *reversed(peers)]:
            pair_arrival(turn, k).wait_recv()
        return jnp.concatenate([gathered(turn, side) for side in range(2)], axis=0)

    with jax.named_scope("s_img0"):
        spread(0, image_of(projected))
    with jax.named_scope("s_rs0"):
        total(0)
    with jax.named_scope("s_ag0"):
        collect(0)
    with jax.named_scope("s_img1"):
        image = gathered(0, core)
        projected = []
        for side in range(2):
            terms = [
                mm_nt(image[:, part * width : (part + 1) * width], cells(part, side)) for part in range(n_gx)
            ]
            projected.append(sum(terms[1:], terms[0]))
        spread(1, image_of(projected))
    with jax.named_scope("s_rs1"):
        total(1)
    with jax.named_scope("s_chol0"):
        image = whole(0)
        inverse = inverse_cholesky(mm_nt(image, image))
    with jax.named_scope("s_ag1"):
        collect(1)
    with jax.named_scope("s_pair1"):
        image = whole(1)
    with jax.named_scope("s_chol1"):
        image = mm(inverse, image)
        inverse = inverse_cholesky(mm_nt(image, image))
        raw = None
        for part in range(n_gx):
            term = mm_nt(cells(part, 0), image[:, part * width : (part + 1) * width])
            raw = term if raw is None else raw + term
        truncated = mm_nt(raw, inverse)

    share = cells_z // n
    for s in range(species):
        for line in range(lines):
            at = (s * lines + line) * cells_z
            core_out[:, line, s * rank : (s + 1) * rank] = truncated[at : at + cells_z]

    spot = my_yz * n_gx + my_x

    def core_copy(k):
        peer = partner(k)
        return remote(
            core_out.at[pl.ds(peer * share, share)], core_ref.at[spot], core_send.at[k - 1], core_recv.at[k - 1], k
        )

    def core_arrival(k):
        source = partner(k)
        spot_of = lax.rem(source, n_yz) * n_gx + lax.div(source, n_yz)
        return remote(
            core_out.at[pl.ds(source * share, share)],
            core_ref.at[spot_of],
            core_send.at[k - 1],
            core_recv.at[k - 1],
            k,
        )

    everyone = range(n - 1, 0, -1)
    with jax.named_scope("s_a2astart"):
        for k in everyone:
            core_copy(k).start()
    with jax.named_scope("s_factor"):
        core_ref[spot] = core_out[pl.ds(me * share, share)]
        factor_ref[...] = mm(inverse, image)
    with jax.named_scope("s_drain"):
        for copy in x_copies:
            copy.wait_send()
        for copy in [*relays, kept_copy]:
            copy.wait_send()
        for turn in range(2):
            for k in peers:
                sum_copy(turn, k).wait_send()
                all_copy(turn, k).wait_send()
                pair_copy(turn, k).wait_send()
            pair_copy(turn, 0).wait_send()
    with jax.named_scope("s_a2await"):
        for k in everyone:
            core_arrival(k).wait()


def finish(core_in, factor_in, core_hbm, factor_hbm, core_buf, sem):
    lines = core_in.shape[2]
    factor_copy = pltpu.make_async_copy(factor_in, factor_hbm, sem.at[0])
    factor_copy.start()
    for spot in range(core_in.shape[0]):
        core_buf[:, spot * lines : (spot + 1) * lines] = core_in[spot]
    core_copy = pltpu.make_async_copy(core_buf, core_hbm, sem.at[1])
    core_copy.start()
    factor_copy.wait()
    core_copy.wait()


def kernel_program(tensor, start_basis, n_gx, n_yz, rows):
    n = n_gx * n_yz
    species, width, lines_held, cells_z = tensor.shape
    rank, total = start_basis.shape
    half = rank // 2
    lines = lines_held // n_gx
    cell_count = species * lines_held * n_yz * cells_z
    share = cells_z // n
    out = species * rank
    owners = n // 2
    dma = pltpu.SemaphoreType.DMA
    core, factor = pl.pallas_call(
        functools.partial(kernel, (n_gx, n_yz, cell_count)),
        out_shape=(
            pltpu.VMEM((n, share, lines, out), jnp.float32),
            pltpu.VMEM((rank, total), jnp.float32),
        ),
        in_specs=[pl.BlockSpec(memory_space=pltpu.HBM)] * 2,
        out_specs=(pl.BlockSpec(memory_space=pltpu.VMEM),) * 2,
        scratch_shapes=[
            pltpu.VMEM((n_gx, 2, species, lines, cells_z, width), jnp.float32),
            pltpu.VMEM((n_gx, half, width), jnp.float32),
            pltpu.VMEM((2, owners, rows, LANES), jnp.float32),
            pltpu.VMEM((2, owners - 1, rows, LANES), jnp.float32),
            pltpu.VMEM((2, 2, owners, rows, LANES), jnp.float32),
            pltpu.VMEM((cells_z, lines, out), jnp.float32),
            dma((1 + n_gx,)),
            dma((species,)),
            dma((species,)),
            dma((species + 1,)),
            dma((species + 1,)),
            dma((2, owners - 1)),
            dma((2, owners - 1)),
            dma((2, owners - 1)),
            dma((2, owners - 1)),
            dma((2, owners)),
            dma((2, owners)),
            dma((n - 1,)),
            dma((n - 1,)),
        ],
        compiler_params=pltpu.CompilerParams(collective_id=0, has_side_effects=True),
    )(tensor.transpose(0, 2, 3, 1), start_basis)
    return pl.pallas_call(
        finish,
        out_shape=(
            jax.ShapeDtypeStruct((share, n * lines, out), jnp.float32),
            jax.ShapeDtypeStruct((rank, total), jnp.float32),
        ),
        in_specs=[pl.BlockSpec(memory_space=pltpu.VMEM)] * 2,
        out_specs=(pl.BlockSpec(memory_space=pltpu.HBM),) * 2,
        scratch_shapes=[pltpu.VMEM((share, n * lines, out), jnp.float32), dma((2,))],
        compiler_params=pltpu.CompilerParams(vmem_limit_bytes=4 << 20),
    )(core, factor)


def orthonormal(image_rows):
    small_gram = jnp.dot(image_rows, image_rows.T, precision=HIGHEST)
    lower_factor = jnp.linalg.cholesky(small_gram)
    return lax.linalg.triangular_solve(lower_factor, image_rows, left_side=True, lower=True)


def collective_program(tensor, start_basis):
    regrouped = lax.all_to_all(tensor, "gx", split_axis=2, concat_axis=1, tiled=True)
    species, _, lines, cells_z = regrouped.shape
    cell_count = species * lines * lax.axis_size("gx") * lax.axis_size("yz") * cells_z
    gram_matrix = lax.dot_general(
        regrouped, regrouped, (((0, 2, 3), (0, 2, 3)), ((), ())), precision=HIGHEST
    )
    gram_matrix = lax.psum(gram_matrix, ("gx", "yz")) / cell_count
    basis = start_basis
    for _ in range(2):
        basis = orthonormal(jnp.dot(basis, gram_matrix, precision=HIGHEST))
    core_local = jnp.einsum("kx,sxyz->zysk", basis, regrouped, precision=HIGHEST)
    core_local = core_local.reshape(cells_z, lines, species * basis.shape[0])
    core_tensor = lax.all_to_all(
        lax.all_to_all(core_local, "gx", split_axis=0, concat_axis=1, tiled=True),
        "yz",
        split_axis=0,
        concat_axis=1,
        tiled=True,
    )
    return core_tensor, basis


def solution(mesh):
    n_gx, n_yz = mesh.shape["gx"], mesh.shape["yz"]
    n = n_gx * n_yz

    def local(tensor, start_basis):
        species, width, lines_held, cells_z = tensor.shape
        rank, total = start_basis.shape
        half, owners = rank // 2, n // 2
        fits = n_gx == 2 and n_yz % 2 == 0 and n & (n - 1) == 0 and rank % (2 * SUBLANES) == 0
        fits = fits and width % LANES == 0 and lines_held % n_gx == 0 and cells_z % max(n, SUBLANES) == 0
        fits = fits and species * width * lines_held * cells_z <= 1 << 19
        rows, left_over = divmod(half * (total // LANES), owners)
        if fits and left_over == 0 and rows and half % rows == 0:
            return kernel_program(tensor, start_basis, n_gx, n_yz, rows)
        return collective_program(tensor, start_basis)

    return jax.shard_map(
        local,
        mesh=mesh,
        in_specs=(P(None, "gx", "yz", None), P()),
        out_specs=(P(("gx", "yz"), None, None), P()),
        check_vma=False,
    )
```

time: 48.7 us -> 45.1 us (0.926)
  Pallas kernels: 46.6 us -> 44.3 us
  local copies, waits for them, and re-layouts: 1.3 us -> 0 us
    pallas_call x1 -> x2, Pallas kernels: 46.6 us -> 44.3 us  [the longest x1 43.6 us: kernel_program(): pl.pallas_call(functools.partial(kernel, (n_gx, n_yz, cell_count)), out_s...]
    unnamed x2 -> x0, local copies, waits for them, and re-layouts: 1.3 us -> none
where the time goes in v1:
time: 45.1 us; the launch traced here: 44.9 us
  Pallas kernels  44.3 us (98%)
  between operations  0.64 us (1%)
    pallas_call x1, Pallas kernels, kernel_program(): pl.pallas_call(functools.partial(kernel, (n_gx, n_yz, cell_count)), out_s...  43.6 us

profile of v1, /device:TPU:0, one launch (start us, length us, event | category | flops | bytes accessed | tf_op | source)
XLA Modules:
  0.0 44.9 jit_solution(11472177117619341492)
XLA Ops:
  0.6 43.6 %shard_map.41 = (f32[32,1,1,384]{3,2,1,0:T(1,128)S(1)}, f32[96,512]{1,0:T(8,128)S(1)}) custom-call(f32[4,2,32,256]{3,2,1,0:T(8,128)} %bitcast.1, f32[96,512]{1,0:T(8,128)} %start_hbm.1), custom_call_target="tpu_custom_call" | custom-call | tf_op jit(solution)/shard_map/pallas_call | solution.py:356
  44.2 0.7 %shard_map.42 = (f32[1,32,384]{2,1,0:T(8,128)}, f32[96,512]{1,0:T(8,128)}) custom-call(f32[32,1,1,384]{3,2,1,0:T(1,128)S(1)} %get-tuple-element.4.core_in, f32[96,512]{1,0:T(8,128)S(1)} %get-tuple-element.5.factor_in), custom_call_target="tpu_custom_call" | custom-call | tf_op jit(solution)/shard_map/pallas_call | solution.py:387

commit v2 on v1

--- a/solution.py
+++ b/solution.py
@@ -69,17 +69,12 @@
     sums,
     core_out,
     local_sem,
-    x_send,
+    send_sem,
     x_recv,
-    relay_send,
     relay_recv,
-    sum_send,
     sum_recv,
-    all_send,
     all_recv,
-    pair_send,
     pair_recv,
-    core_send,
     core_recv,
 ):
     n_gx, n_yz, cell_count = shape
@@ -106,8 +101,16 @@
 
     def remote(src, dst, send, recv, k):
         return pltpu.make_async_remote_copy(
-            src_ref=src, dst_ref=dst, send_sem=send, recv_sem=recv, device_id=place(partner(k)), device_id_type=MESH
+            src_ref=src,
+            dst_ref=dst,
+            send_sem=send_sem.at[send],
+            recv_sem=recv,
+            device_id=place(partner(k)),
+            device_id_type=MESH,
         )
+
+    def take(ref, sem):
+        pltpu.make_async_copy(ref, ref, sem).wait()
 
     barrier = pltpu.get_barrier_semaphore()
     across = n_yz
@@ -119,29 +122,17 @@
     own_copy = pltpu.make_async_copy(x_hbm.at[:, kept], xf.at[my_x, 0], local_sem.at[0])
     own_copy.start()
     mine_rows = pl.ds(pl.multiple_of(core * half, SUBLANES), half)
-    start_copies = [
+    for part in range(n_gx):
         pltpu.make_async_copy(
-            start_hbm.at[mine_rows, part * width : (part + 1) * width], start.at[part], local_sem.at[1 + part]
-        )
-        for part in range(n_gx)
-    ]
-    for copy in start_copies:
-        copy.start()
+            start_hbm.at[mine_rows, part * width : (part + 1) * width], start.at[part], local_sem.at[1]
+        ).start()
 
     with jax.named_scope("s_barrier"):
         pl.semaphore_wait(barrier, n - 1)
 
-    x_copies = [
-        remote(x_hbm.at[s, given], xf.at[my_x, 0, s], x_send.at[s], x_recv.at[s], across) for s in range(species)
-    ]
-    x_arrivals = [
-        remote(x_hbm.at[s, given], xf.at[other_x, 0, s], x_send.at[s], x_recv.at[s], across) for s in range(species)
-    ]
-    kept_copy = remote(x_hbm.at[:, kept], xf.at[my_x, 1], relay_send.at[species], relay_recv.at[species], 1)
-    relays = [
-        remote(xf.at[other_x, 0, s], xf.at[other_x, 1, s], relay_send.at[s], relay_recv.at[s], 1)
-        for s in range(species)
-    ]
+    x_copies = [remote(x_hbm.at[s, given], xf.at[my_x, 0, s], 0, x_recv.at[s], across) for s in range(species)]
+    kept_copy = remote(x_hbm.at[:, kept], xf.at[my_x, 1], 1, relay_recv.at[0], 1)
+    relays = [remote(xf.at[other_x, 0, s], xf.at[other_x, 1, s], 1, relay_recv.at[1], 1) for s in range(species)]
 
     def cells(part, side):
         return xf[part, side].reshape(held_cells, width)
@@ -151,16 +142,14 @@
             copy.start()
         kept_copy.start()
         own_copy.wait()
-        for copy in start_copies:
-            copy.wait()
-        kept_copy.wait_recv()
+        take(start, local_sem.at[1])
+        take(xf.at[my_x, 1], relay_recv.at[0])
         projected = [mm_nt(start[my_x], cells(my_x, side)) for side in range(2)]
-        for arrival, relay in zip(x_arrivals, relays):
-            arrival.wait_recv()
+        for s, relay in enumerate(relays):
+            take(xf.at[other_x, 0, s], x_recv.at[s])
             relay.start()
         projected[0] = projected[0] + mm_nt(start[other_x], cells(other_x, 0))
-        for relay in relays:
-            relay.wait_recv()
+        take(xf.at[other_x, 1], relay_recv.at[1])
         projected[1] = projected[1] + mm_nt(start[other_x], cells(other_x, 1))
 
     def image_of(projected):
@@ -169,51 +158,16 @@
         return jnp.concatenate(columns, axis=1)
 
     def sum_copy(turn, k):
-        return remote(
-            stage.at[turn, lax.div(partner(k), 2)],
-            parts.at[turn, k // 2 - 1],
-            sum_send.at[turn, k // 2 - 1],
-            sum_recv.at[turn, k // 2 - 1],
-            k,
-        )
+        block = lax.div(partner(k), 2)
+        return remote(stage.at[turn, block], parts.at[turn, k // 2 - 1], 2 + turn, sum_recv.at[turn], k)
 
     def all_copy(turn, k):
-        return remote(
-            sums.at[turn, core, mine],
-            sums.at[turn, core, mine],
-            all_send.at[turn, k // 2 - 1],
-            all_recv.at[turn, k // 2 - 1],
-            k,
-        )
-
-    def all_arrival(turn, k):
-        return remote(
-            sums.at[turn, core, mine],
-            sums.at[turn, core, lax.div(partner(k), 2)],
-            all_send.at[turn, k // 2 - 1],
-            all_recv.at[turn, k // 2 - 1],
-            k,
-        )
+        block = sums.at[turn, core, mine]
+        return remote(block, block, 4 + turn, all_recv.at[k // 2 if turn else 0], k)
 
     def pair_copy(turn, k):
-        block = lax.div(partner(k), 2)
-        return remote(
-            sums.at[turn, core, block],
-            sums.at[turn, core, block],
-            pair_send.at[turn, k // 2],
-            pair_recv.at[turn, k // 2],
-            1,
-        )
-
-    def pair_arrival(turn, k):
-        block = lax.div(partner(k), 2)
-        return remote(
-            sums.at[turn, core, block],
-            sums.at[turn, 1 - core, block],
-            pair_send.at[turn, k // 2],
-            pair_recv.at[turn, k // 2],
-            1,
-        )
+        block = sums.at[turn, core, lax.div(partner(k), 2)]
+        return remote(block, block, 7, pair_recv.at[1], 1)
 
     def spread(turn, image):
         for owner in range(owners):
@@ -223,30 +177,23 @@
             sum_copy(turn, k).start()
 
     def total(turn):
-        terms = [stage[turn, mine]]
-        for k in reversed(peers):
-            sum_copy(turn, k).wait_recv()
-            terms.append(parts[turn, k // 2 - 1])
+        take(parts.at[turn], sum_recv.at[turn])
+        terms = [stage[turn, mine]] + [parts[turn, k // 2 - 1] for k in peers]
         while len(terms) > 1:
             terms = [a + b for a, b in zip(terms[::2], terms[1::2])] + ([terms[-1]] if len(terms) % 2 else [])
         sums[turn, core, mine] = terms[0]
         for k in peers:
             all_copy(turn, k).start()
-        pair_copy(turn, 0).start()
 
     def gathered(turn, side):
         blocks = [sums[turn, side, owner] for owner in range(owners)]
         columns = [jnp.concatenate(blocks[at : at + per_column], axis=0) for at in range(0, owners, per_column)]
         return jnp.concatenate(columns, axis=1)
 
-    def collect(turn):
-        for k in reversed(peers):
-            all_arrival(turn, k).wait_recv()
-            pair_copy(turn, k).start()
+    held = pl.ds(0, owners - 1)
 
     def whole(turn):
-        for k in [0, *reversed(peers)]:
-            pair_arrival(turn, k).wait_recv()
+        take(sums.at[turn, 1 - core], pair_recv.at[turn])
         return jnp.concatenate([gathered(turn, side) for side in range(2)], axis=0)
 
     with jax.named_scope("s_img0"):
@@ -254,7 +201,9 @@
     with jax.named_scope("s_rs0"):
         total(0)
     with jax.named_scope("s_ag0"):
-        collect(0)
+        take(sums.at[0, core, held], all_recv.at[0])
+        pair_all = remote(sums.at[0, core], sums.at[0, core], 6, pair_recv.at[0], 1)
+        pair_all.start()
     with jax.named_scope("s_img1"):
         image = gathered(0, core)
         projected = []
@@ -270,7 +219,10 @@
         image = whole(0)
         inverse = inverse_cholesky(mm_nt(image, image))
     with jax.named_scope("s_ag1"):
-        collect(1)
+        pair_copy(1, 0).start()
+        for k in reversed(peers):
+            take(sums.at[1, core, mine], all_recv.at[k // 2])
+            pair_copy(1, k).start()
     with jax.named_scope("s_pair1"):
         image = whole(1)
     with jax.named_scope("s_chol1"):
@@ -292,20 +244,7 @@
 
     def core_copy(k):
         peer = partner(k)
-        return remote(
-            core_out.at[pl.ds(peer * share, share)], core_ref.at[spot], core_send.at[k - 1], core_recv.at[k - 1], k
-        )
-
-    def core_arrival(k):
-        source = partner(k)
-        spot_of = lax.rem(source, n_yz) * n_gx + lax.div(source, n_yz)
-        return remote(
-            core_out.at[pl.ds(source * share, share)],
-            core_ref.at[spot_of],
-            core_send.at[k - 1],
-            core_recv.at[k - 1],
-            k,
-        )
+        return remote(core_out.at[pl.ds(peer * share, share)], core_ref.at[spot], 8, core_recv.at[0], k)
 
     everyone = range(n - 1, 0, -1)
     with jax.named_scope("s_a2astart"):
@@ -315,19 +254,16 @@
         core_ref[spot] = core_out[pl.ds(me * share, share)]
         factor_ref[...] = mm(inverse, image)
     with jax.named_scope("s_drain"):
-        for copy in x_copies:
-            copy.wait_send()
-        for copy in [*relays, kept_copy]:
-            copy.wait_send()
+        take(xf.at[my_x, 0], send_sem.at[0])
+        for side in range(2):
+            take(xf.at[my_x, side], send_sem.at[1])
         for turn in range(2):
-            for k in peers:
-                sum_copy(turn, k).wait_send()
-                all_copy(turn, k).wait_send()
-                pair_copy(turn, k).wait_send()
-            pair_copy(turn, 0).wait_send()
+            take(parts.at[turn], send_sem.at[2 + turn])
+            take(parts.at[turn], send_sem.at[4 + turn])
+            take(sums.at[turn, core], send_sem.at[6 + turn])
+        take(core_ref.at[pl.ds(0, n - 1)], send_sem.at[8])
     with jax.named_scope("s_a2await"):
-        for k in everyone:
-            core_arrival(k).wait()
+        take(core_ref.at[pl.ds(0, n - 1)], core_recv.at[0])
 
 
 def finish(core_in, factor_in, core_hbm, factor_hbm, core_buf, sem):
@@ -368,19 +304,14 @@
             pltpu.VMEM((2, owners - 1, rows, LANES), jnp.float32),
             pltpu.VMEM((2, 2, owners, rows, LANES), jnp.float32),
             pltpu.VMEM((cells_z, lines, out), jnp.float32),
-            dma((1 + n_gx,)),
+            dma((2,)),
+            dma((9,)),
             dma((species,)),
-            dma((species,)),
-            dma((species + 1,)),
-            dma((species + 1,)),
-            dma((2, owners - 1)),
-            dma((2, owners - 1)),
-            dma((2, owners - 1)),
-            dma((2, owners - 1)),
-            dma((2, owners)),
-            dma((2, owners)),
-            dma((n - 1,)),
-            dma((n - 1,)),
+            dma((2,)),
+            dma((2,)),
+            dma((owners,)),
+            dma((2,)),
+            dma((1,)),
         ],
         compiler_params=pltpu.CompilerParams(collective_id=0, has_side_effects=True),
     )(tensor.transpose(0, 2, 3, 1), start_basis)

time: 45.1 us -> 42.9 us (0.951)
  Pallas kernels: 44.3 us -> 42.1 us
    pallas_call x1, Pallas kernels: 43.6 us -> 41.4 us  [kernel_program(): pl.pallas_call(functools.partial(kernel, (n_gx, n_yz, cell_count)), out_s...]
where the time goes in v2:
time: 42.9 us; the launch traced here: 42.7 us
  Pallas kernels  42.1 us (98%)
  between operations  0.64 us (1%)
    pallas_call x1, Pallas kernels, kernel_program(): pl.pallas_call(functools.partial(kernel, (n_gx, n_yz, cell_count)), out_s...  41.4 us

profile of v2, /device:TPU:0, one launch (start us, length us, event | category | flops | bytes accessed | tf_op | source)
XLA Modules:
  0.0 42.7 jit_solution(2968437529028189995)
XLA Ops:
  0.6 41.4 %shard_map.41 = (f32[32,1,1,384]{3,2,1,0:T(1,128)S(1)}, f32[96,512]{1,0:T(8,128)S(1)}) custom-call(f32[4,2,32,256]{3,2,1,0:T(8,128)} %bitcast.1, f32[96,512]{1,0:T(8,128)} %start_hbm.1), custom_call_target="tpu_custom_call" | custom-call | tf_op jit(solution)/shard_map/pallas_call | solution.py:292
  42.0 0.7 %shard_map.42 = (f32[1,32,384]{2,1,0:T(8,128)}, f32[96,512]{1,0:T(8,128)}) custom-call(f32[32,1,1,384]{3,2,1,0:T(1,128)S(1)} %get-tuple-element.4.core_in, f32[96,512]{1,0:T(8,128)S(1)} %get-tuple-element.5.factor_in), custom_call_target="tpu_custom_call" | custom-call | tf_op jit(solution)/shard_map/pallas_call | solution.py:318

commit v3 on v2

--- a/solution.py
+++ b/solution.py
@@ -25,35 +25,48 @@
     )
 
 
-def inverse_cholesky(gram, panel=SUBLANES):
+def inverse_cholesky(gram, panel=2 * SUBLANES):
     rank = gram.shape[0]
     wide = -(-rank // LANES) * LANES
-    row_id = lax.broadcasted_iota(jnp.int32, (rank, wide), 0)
-    lane_id = lax.broadcasted_iota(jnp.int32, (rank, wide), 1)
+    row_id = lax.broadcasted_iota(jnp.int32, (SUBLANES, wide), 0)
+    lane_id = lax.broadcasted_iota(jnp.int32, (SUBLANES, wide), 1)
     left = jnp.concatenate([gram, jnp.zeros((rank, wide - rank), jnp.float32)], axis=1) if wide > rank else gram
-    right = jnp.where(row_id == lane_id, 1.0, 0.0).astype(jnp.float32)
-    done_right = []
-    for base in range(0, rank, SUBLANES):
-        rows = rank - base
-        local_row = lax.broadcasted_iota(jnp.int32, (rows, wide), 0)
-        pivots = jnp.zeros((SUBLANES, wide), jnp.float32)
-        for first in range(0, SUBLANES, panel):
-            spread = [
-                jnp.broadcast_to(left[:, base + step : base + step + 1], (rows, wide))
-                for step in range(first, first + panel)
-            ]
-            for step in range(first, first + panel):
-                column = spread[step - first]
-                pivot = column[step : step + 1]
-                pivots = jnp.where(local_row[:SUBLANES] == step, jnp.broadcast_to(pivot, (SUBLANES, wide)), pivots)
-                factor = jnp.where(local_row > step, column * (1.0 / pivot), 0.0)
-                for other in range(step + 1, first + panel):
-                    spread[other - first] = spread[other - first] - factor * spread[other - first][step : step + 1]
-                left = left - factor * left[step : step + 1]
-                right = right - factor * right[step : step + 1]
-        done_right.append(right[:SUBLANES] / jnp.sqrt(pivots))
-        left, right = left[SUBLANES:], right[SUBLANES:]
-    return jnp.concatenate(done_right, axis=0)[:, :rank]
+    count = rank // SUBLANES
+    left = [left[i * SUBLANES : (i + 1) * SUBLANES] for i in range(count)]
+    done = []
+    for base in range(0, rank, panel):
+        at = base // SUBLANES
+        spread = [
+            {
+                i: jnp.broadcast_to(left[i][:, base + c : base + c + 1], (SUBLANES, wide))
+                for i in range(at + c // SUBLANES, count)
+            }
+            for c in range(panel)
+        ]
+        inside = (lane_id >= base) & (lane_id < base + panel)
+        for i in range(at, count):
+            unit = jnp.where(row_id + i * SUBLANES == lane_id, 1.0, 0.0) if i < at + panel // SUBLANES else 0.0
+            left[i] = jnp.where(inside, unit, left[i])
+        for c in range(panel):
+            block, row = at + c // SUBLANES, c % SUBLANES
+            pivot = spread[c][block][row : row + 1]
+            scale = 1.0 / pivot
+            tall = jnp.broadcast_to(pivot, (SUBLANES, wide))
+            pivots = tall if row == 0 else jnp.where(row_id == row, tall, pivots)
+            factor = {i: spread[c][i] * scale for i in range(block, count)}
+            factor[block] = jnp.where(row_id > row, factor[block], 0.0)
+            for later in range(c + 1, panel):
+                first, sub = at + later // SUBLANES, later % SUBLANES
+                value = spread[c][first][sub : sub + 1]
+                for i in range(first, count):
+                    spread[later][i] = spread[later][i] - factor[i] * value
+            pivot_row = left[block][row : row + 1]
+            for i in range(block, count):
+                left[i] = left[i] - factor[i] * pivot_row
+            if row == SUBLANES - 1:
+                lower = jnp.where(lane_id <= row_id + block * SUBLANES, left[block], 0.0)
+                done.append(lower / jnp.sqrt(pivots))
+    return jnp.concatenate(done, axis=0)[:, :rank]
 
 
 def kernel(
@@ -62,16 +75,22 @@
     start_hbm,
     core_ref,
     factor_ref,
+    xa,
     xf,
     start,
+    product,
+    product_in,
+    stage0,
+    parts0,
     stage,
     parts,
     sums,
     core_out,
+    news_sem,
     local_sem,
     send_sem,
-    x_recv,
-    relay_recv,
+    cell_recv,
+    product_recv,
     sum_recv,
     all_recv,
     pair_recv,
@@ -85,13 +104,16 @@
     mine = lax.div(me, 2)
     other_x = 1 - my_x
     _, _, species, lines, cells_z, width = xf.shape
-    half = start.shape[1]
+    half = start.shape[0]
     rank = 2 * half
-    owners, rows = stage.shape[1:3]
+    owners, rows = stage.shape[:2]
     per_column = half // rows
     held_cells = species * lines * cells_z
     flips = [1 - 2 * lax.rem(lax.div(me, 1 << bit), 2) for bit in range(n.bit_length() - 1)]
     peers = range(n - 2, 0, -2)
+    near_peers = range(n_yz - 2, 0, -2)
+    near_owners = n_yz // 2
+    near_mine = lax.div(my_yz, 2)
 
     def place(flat):
         return {"gx": lax.div(flat, n_yz), "yz": lax.rem(flat, n_yz)}
@@ -114,71 +136,84 @@
 
     barrier = pltpu.get_barrier_semaphore()
     across = n_yz
-    for k in [across, 1, *(k for k in range(n - 1, 0, -1) if k not in (across, 1))]:
+    bits = [1, across, *(1 << bit for bit in range(1, n_yz.bit_length() - 1))]
+    for k in bits:
         pl.semaphore_signal(barrier, inc=1, device_id=place(partner(k)), device_id_type=MESH)
 
+    own_copy = pltpu.make_async_copy(x_hbm, xa.at[0], local_sem.at[0])
+    own_copy.start()
+    mine_rows = pl.ds(pl.multiple_of(core * half, SUBLANES), half)
+    mine_columns = pl.ds(pl.multiple_of(my_x * width, LANES), width)
+    start_copy = pltpu.make_async_copy(start_hbm.at[mine_rows, mine_columns], start, local_sem.at[1])
+    start_copy.start()
     kept = pl.ds(my_x * lines, lines)
     given = pl.ds(other_x * lines, lines)
-    own_copy = pltpu.make_async_copy(x_hbm.at[:, kept], xf.at[my_x, 0], local_sem.at[0])
-    own_copy.start()
-    mine_rows = pl.ds(pl.multiple_of(core * half, SUBLANES), half)
-    for part in range(n_gx):
-        pltpu.make_async_copy(
-            start_hbm.at[mine_rows, part * width : (part + 1) * width], start.at[part], local_sem.at[1]
-        ).start()
+    kept_copy = pltpu.make_async_copy(x_hbm.at[:, kept], xf.at[my_x, 0], local_sem.at[2])
+    kept_copy.start()
 
     with jax.named_scope("s_barrier"):
-        pl.semaphore_wait(barrier, n - 1)
-
-    x_copies = [remote(x_hbm.at[s, given], xf.at[my_x, 0, s], 0, x_recv.at[s], across) for s in range(species)]
-    kept_copy = remote(x_hbm.at[:, kept], xf.at[my_x, 1], 1, relay_recv.at[0], 1)
-    relays = [remote(xf.at[other_x, 0, s], xf.at[other_x, 1, s], 1, relay_recv.at[1], 1) for s in range(species)]
+        pl.semaphore_wait(barrier, len(bits))
+
+    pair_cells = remote(x_hbm, xa.at[1], 0, cell_recv.at[0], 1)
+    x_copy = remote(x_hbm.at[:, given], xf.at[my_x, 0], 1, cell_recv.at[1], across)
+    relay = remote(xf.at[other_x, 0], xf.at[other_x, 1], 2, cell_recv.at[2], 1)
+    pair_kept = pltpu.make_async_copy(xa.at[1, :, kept], xf.at[my_x, 1], local_sem.at[3])
 
     def cells(part, side):
         return xf[part, side].reshape(held_cells, width)
 
+    def half_cells(side):
+        return xa[side].reshape(n_gx * held_cells, width)
+
+    def send_product(side):
+        product[side] = mm_nt(start[...], half_cells(side)) * (1.0 / cell_count)
+        remote(product.at[side], product_in.at[side], 3, product_recv.at[side], across).start()
+
     with jax.named_scope("s_xex"):
-        for copy in x_copies:
-            copy.start()
-        kept_copy.start()
+        pair_cells.start()
         own_copy.wait()
-        take(start, local_sem.at[1])
-        take(xf.at[my_x, 1], relay_recv.at[0])
-        projected = [mm_nt(start[my_x], cells(my_x, side)) for side in range(2)]
-        for s, relay in enumerate(relays):
-            take(xf.at[other_x, 0, s], x_recv.at[s])
-            relay.start()
-        projected[0] = projected[0] + mm_nt(start[other_x], cells(other_x, 0))
-        take(xf.at[other_x, 1], relay_recv.at[1])
-        projected[1] = projected[1] + mm_nt(start[other_x], cells(other_x, 1))
+        start_copy.wait()
+        send_product(0)
+        take(xa.at[1], cell_recv.at[0])
+        send_product(1)
+        pair_kept.start()
+    with jax.named_scope("s_news"):
+        for i, k in enumerate(bits):
+            pl.semaphore_signal(news_sem.at[i], inc=1, device_id=place(partner(k)), device_id_type=MESH)
+            pl.semaphore_wait(news_sem.at[i], 1)
+    with jax.named_scope("s_prod"):
+        image = None
+        for side in range(2):
+            take(product_in.at[side], product_recv.at[side])
+            term = mm(product[side] + product_in[side], half_cells(side))
+            image = term if image is None else image + term
 
     def image_of(projected):
         projected = [term * (1.0 / cell_count) for term in projected]
         columns = [sum(mm(projected[side], cells(part, side)) for side in range(2)) for part in range(n_gx)]
         return jnp.concatenate(columns, axis=1)
 
-    def sum_copy(turn, k):
-        block = lax.div(partner(k), 2)
-        return remote(stage.at[turn, block], parts.at[turn, k // 2 - 1], 2 + turn, sum_recv.at[turn], k)
+    def near_sum_copy(k):
+        block = lax.div(lax.rem(partner(k), n_yz), 2)
+        return remote(stage0.at[block], parts0.at[k // 2 - 1], 4, sum_recv.at[0], k)
+
+    def sum_copy(k):
+        return remote(stage.at[lax.div(partner(k), 2)], parts.at[k // 2 - 1], 5, sum_recv.at[1], k)
 
     def all_copy(turn, k):
         block = sums.at[turn, core, mine]
-        return remote(block, block, 4 + turn, all_recv.at[k // 2 if turn else 0], k)
+        return remote(block, block, 6 + turn, all_recv.at[k // 2 if turn else 0], k)
 
     def pair_copy(turn, k):
         block = sums.at[turn, core, lax.div(partner(k), 2)]
-        return remote(block, block, 7, pair_recv.at[1], 1)
-
-    def spread(turn, image):
-        for owner in range(owners):
+        return remote(block, block, 9, pair_recv.at[1], 1)
+
+    def spread(buffer, image):
+        for owner in range(buffer.shape[0]):
             column, block = owner // per_column, owner % per_column
-            stage[turn, owner] = image[block * rows : (block + 1) * rows, column * LANES : (column + 1) * LANES]
-        for k in peers:
-            sum_copy(turn, k).start()
-
-    def total(turn):
-        take(parts.at[turn], sum_recv.at[turn])
-        terms = [stage[turn, mine]] + [parts[turn, k // 2 - 1] for k in peers]
+            buffer[owner] = image[block * rows : (block + 1) * rows, column * LANES : (column + 1) * LANES]
+
+    def total(turn, terms):
         while len(terms) > 1:
             terms = [a + b for a, b in zip(terms[::2], terms[1::2])] + ([terms[-1]] if len(terms) % 2 else [])
         sums[turn, core, mine] = terms[0]
@@ -197,24 +232,36 @@
         return jnp.concatenate([gathered(turn, side) for side in range(2)], axis=0)
 
     with jax.named_scope("s_img0"):
-        spread(0, image_of(projected))
+        spread(stage0, image)
+        for k in near_peers:
+            near_sum_copy(k).start()
+        x_copy.start()
     with jax.named_scope("s_rs0"):
-        total(0)
+        take(parts0, sum_recv.at[0])
+        total(0, [stage0[near_mine]] + [parts0[k // 2 - 1] for k in near_peers])
     with jax.named_scope("s_ag0"):
+        take(xf.at[other_x, 0], cell_recv.at[1])
+        relay.start()
         take(sums.at[0, core, held], all_recv.at[0])
-        pair_all = remote(sums.at[0, core], sums.at[0, core], 6, pair_recv.at[0], 1)
+        pair_all = remote(sums.at[0, core], sums.at[0, core], 8, pair_recv.at[0], 1)
         pair_all.start()
     with jax.named_scope("s_img1"):
         image = gathered(0, core)
+        kept_copy.wait()
+        pair_kept.wait()
+        take(xf.at[other_x, 1], cell_recv.at[2])
         projected = []
         for side in range(2):
             terms = [
                 mm_nt(image[:, part * width : (part + 1) * width], cells(part, side)) for part in range(n_gx)
             ]
             projected.append(sum(terms[1:], terms[0]))
-        spread(1, image_of(projected))
+        spread(stage, image_of(projected))
+        for k in peers:
+            sum_copy(k).start()
     with jax.named_scope("s_rs1"):
-        total(1)
+        take(parts, sum_recv.at[1])
+        total(1, [stage[mine]] + [parts[k // 2 - 1] for k in peers])
     with jax.named_scope("s_chol0"):
         image = whole(0)
         inverse = inverse_cholesky(mm_nt(image, image))
@@ -244,7 +291,7 @@
 
     def core_copy(k):
         peer = partner(k)
-        return remote(core_out.at[pl.ds(peer * share, share)], core_ref.at[spot], 8, core_recv.at[0], k)
+        return remote(core_out.at[pl.ds(peer * share, share)], core_ref.at[spot], 10, core_recv.at[0], k)
 
     everyone = range(n - 1, 0, -1)
     with jax.named_scope("s_a2astart"):
@@ -254,14 +301,16 @@
         core_ref[spot] = core_out[pl.ds(me * share, share)]
         factor_ref[...] = mm(inverse, image)
     with jax.named_scope("s_drain"):
-        take(xf.at[my_x, 0], send_sem.at[0])
-        for side in range(2):
-            take(xf.at[my_x, side], send_sem.at[1])
+        take(xa.at[0], send_sem.at[0])
+        take(xf.at[my_x, 0], send_sem.at[1])
+        take(xf.at[other_x, 0], send_sem.at[2])
+        take(product, send_sem.at[3])
+        take(parts0, send_sem.at[4])
+        take(parts, send_sem.at[5])
         for turn in range(2):
-            take(parts.at[turn], send_sem.at[2 + turn])
-            take(parts.at[turn], send_sem.at[4 + turn])
-            take(sums.at[turn, core], send_sem.at[6 + turn])
-        take(core_ref.at[pl.ds(0, n - 1)], send_sem.at[8])
+            take(parts, send_sem.at[6 + turn])
+            take(sums.at[turn, core], send_sem.at[8 + turn])
+        take(core_ref.at[pl.ds(0, n - 1)], send_sem.at[10])
     with jax.named_scope("s_a2await"):
         take(core_ref.at[pl.ds(0, n - 1)], core_recv.at[0])
 
@@ -298,15 +347,21 @@
         in_specs=[pl.BlockSpec(memory_space=pltpu.HBM)] * 2,
         out_specs=(pl.BlockSpec(memory_space=pltpu.VMEM),) * 2,
         scratch_shapes=[
+            pltpu.VMEM((2, species, lines_held, cells_z, width), jnp.float32),
             pltpu.VMEM((n_gx, 2, species, lines, cells_z, width), jnp.float32),
-            pltpu.VMEM((n_gx, half, width), jnp.float32),
-            pltpu.VMEM((2, owners, rows, LANES), jnp.float32),
-            pltpu.VMEM((2, owners - 1, rows, LANES), jnp.float32),
+            pltpu.VMEM((half, width), jnp.float32),
+            pltpu.VMEM((2, half, species * lines_held * cells_z), jnp.float32),
+            pltpu.VMEM((2, half, species * lines_held * cells_z), jnp.float32),
+            pltpu.VMEM((n_yz // 2, rows, LANES), jnp.float32),
+            pltpu.VMEM((n_yz // 2 - 1, rows, LANES), jnp.float32),
+            pltpu.VMEM((owners, rows, LANES), jnp.float32),
+            pltpu.VMEM((owners - 1, rows, LANES), jnp.float32),
             pltpu.VMEM((2, 2, owners, rows, LANES), jnp.float32),
             pltpu.VMEM((cells_z, lines, out), jnp.float32),
-            dma((2,)),
-            dma((9,)),
-            dma((species,)),
+            pltpu.SemaphoreType.REGULAR((n.bit_length() - 1,)),
+            dma((4,)),
+            dma((11,)),
+            dma((3,)),
             dma((2,)),
             dma((2,)),
             dma((owners,)),

time: 42.9 us -> 42.2 us (0.984)
  Pallas kernels: 42.1 us -> 41.4 us
    pallas_call x1, Pallas kernels: 41.4 us -> 40.7 us  [kernel_program(): pl.pallas_call(functools.partial(kernel, (n_gx, n_yz, cell_count)), out_s...]
where the time goes in v3:
time: 42.2 us; the launch traced here: 42 us
  Pallas kernels  41.4 us (98%)
  between operations  0.64 us (2%)
    pallas_call x1, Pallas kernels, kernel_program(): pl.pallas_call(functools.partial(kernel, (n_gx, n_yz, cell_count)), out_s...  40.7 us

profile of v3, /device:TPU:0, one launch (start us, length us, event | category | flops | bytes accessed | tf_op | source)
XLA Modules:
  0.0 42.0 jit_solution(4326209992389613208)
XLA Ops:
  0.6 40.7 %shard_map.41 = (f32[32,1,1,384]{3,2,1,0:T(1,128)S(1)}, f32[96,512]{1,0:T(8,128)S(1)}) custom-call(f32[4,2,32,256]{3,2,1,0:T(8,128)} %bitcast.1, f32[96,512]{1,0:T(8,128)} %start_hbm.1), custom_call_target="tpu_custom_call" | custom-call | tf_op jit(solution)/shard_map/pallas_call | solution.py:341
  41.3 0.7 %shard_map.42 = (f32[1,32,384]{2,1,0:T(8,128)}, f32[96,512]{1,0:T(8,128)}) custom-call(f32[32,1,1,384]{3,2,1,0:T(1,128)S(1)} %get-tuple-element.4.core_in, f32[96,512]{1,0:T(8,128)S(1)} %get-tuple-element.5.factor_in), custom_call_target="tpu_custom_call" | custom-call | tf_op jit(solution)/shard_map/pallas_call | solution.py:373
